TPU v7x, 32 devices: a whole 2x2x4 slice. The times are simulated.
32 devices in a mesh: parts: 2 (over y), tok: 4 (over z), head: 2 (over x), rep: 2 (over core).
Axes of the slice: x: 2, y: 2, z: 4, core: 2. Of those that a mesh axis runs over, the one named last changes fastest.
Arguments:
- keys: bfloat16 [12288, 4096], P(('parts', 'tok'), 'head'), parts along dimension 0, may hold values from -6 to 6
- values: bfloat16 [12288, 4096], P(('parts', 'tok'), 'head'), parts along dimension 0, may hold values from -6 to 6
- queries: bfloat16 [12288, 4096], P(('parts', 'tok'), 'head'), parts along dimension 0, may hold values from -6 to 6
- next_queries: bfloat16 [12288, 4096], P(('parts', 'tok'), 'head'), parts along dimension 0, may hold values from -6 to 6
- rates: bfloat16 [12288, 8], P(('parts', 'tok'), 'head'), parts along dimension 0, may hold values from 0.099609375 to 1
- tile_counts: int32 [8], P(('parts', 'tok')), parts along dimension 0, may hold values from 1 to 12, as said below
- w_gate: bfloat16 [8, 512, 512], P('head', None, 'rep'), may hold values from -0.25 to 0.25
- w_up: bfloat16 [8, 512, 512], P('head', None, 'rep'), may hold values from -0.25 to 0.25
- w_down: bfloat16 [8, 512, 512], P('head', 'rep'), may hold values from -0.25 to 0.25
Outputs:
- out_block: bfloat16 [12288, 4096], P(('parts', 'tok'), ('head', 'rep')), parts along dimension 0
- out_next: bfloat16 [12288, 4096], P(('parts', 'tok'), ('head', 'rep')), parts along dimension 0
There are 2 independent parts, one for each index of `parts`. A program takes and returns all parts, laid end to end along the dimension named above; an argument that names none is the same for every part. Nothing has to cross between parts.
Inputs may be any that keep to these rules, and one draw needn't show every extreme that they name: tile_counts[i] counts the leading 128-token tiles of token shard i whose tokens are valid; in every draw some shard has all 12 tiles valid.
All inputs are finite; a program needn't handle non-finite values.
Results may differ from a plain program's by a relative error of at most 0.0085.
Values may be sent and summed in bfloat16 or wider, within the bound.
A program may use at most 192 MiB of HBM per device.

v0:
```python
import jax
import jax.numpy as jnp
from jax import lax
from jax.sharding import PartitionSpec as P

TILE = 128


def tile_grads(key_tiles, value_tiles, rate_tiles, own_load, gate_w, up_w, down_w):

    def tile_step(tile_pos, totals):
        key_tile = lax.dynamic_index_in_dim(key_tiles, tile_pos, 0, keepdims=False)
        value_tile = lax.dynamic_index_in_dim(value_tiles, tile_pos, 0, keepdims=False)
        eta_tile = lax.dynamic_index_in_dim(rate_tiles, tile_pos, 0, keepdims=False).astype(
            jnp.float32
        )[..., None]
        gate_pre = jnp.einsum("tgd,gdf->tgf", key_tile, gate_w, preferred_element_type=jnp.float32)
        up_pre = jnp.einsum("tgd,gdf->tgf", key_tile, up_w, preferred_element_type=jnp.float32)
        sigma_gate = jax.nn.sigmoid(gate_pre)
        silu_gate = gate_pre * sigma_gate
        hidden_rows = (eta_tile * silu_gate * up_pre).astype(jnp.bfloat16)
        down_part = jnp.einsum(
            "tgf,tgd->gfd", hidden_rows, value_tile, preferred_element_type=jnp.float32
        )
        back_hidden = jnp.einsum(
            "tgd,gfd->tgf", value_tile, down_w, preferred_element_type=jnp.float32
        )
        slope = sigma_gate * (1.0 + gate_pre * (1.0 - sigma_gate))
        gate_err = (eta_tile * back_hidden * up_pre * slope).astype(jnp.bfloat16)
        up_err = (eta_tile * back_hidden * silu_gate).astype(jnp.bfloat16)
        gate_part = jnp.einsum(
            "tgd,tgf->gdf", key_tile, gate_err, preferred_element_type=jnp.float32
        )
        up_part = jnp.einsum("tgd,tgf->gdf", key_tile, up_err, preferred_element_type=jnp.float32)
        return (totals[0] + gate_part, totals[1] + up_part, totals[2] + down_part)

    start_sums = (
        jnp.zeros(gate_w.shape, jnp.float32),
        jnp.zeros(up_w.shape, jnp.float32),
        jnp.zeros(down_w.shape, jnp.float32),
    )
    return lax.fori_loop(0, own_load, tile_step, start_sums)


def renorm_local(weight, change, axis_pos, step_scale):
    weight_f = weight.astype(jnp.float32)
    updated = weight_f + step_scale * change
    target = jnp.sqrt(jnp.sum(weight_f * weight_f, axis=axis_pos, keepdims=True))
    current = jnp.sqrt(jnp.sum(updated * updated, axis=axis_pos, keepdims=True) + 1e-06)
    return (updated * (target / current)).astype(jnp.bfloat16)


def new_weights(gradients, gate_w, up_w, down_w, step_scale):
    summed = lax.psum((gradients[0], gradients[1], gradients[2]), "tok")
    return (
        renorm_local(gate_w, summed[0], 1, step_scale),
        renorm_local(up_w, summed[1], 1, step_scale),
        renorm_local(down_w, summed[2], 2, step_scale),
    )


def forward_rows(query_rows, gate_w, up_w, down_w):
    gate_pre = jnp.einsum("ngd,gdf->ngf", query_rows, gate_w, preferred_element_type=jnp.float32)
    up_pre = jnp.einsum("ngd,gdf->ngf", query_rows, up_w, preferred_element_type=jnp.float32)
    hidden_rows = (jax.nn.silu(gate_pre) * up_pre).astype(jnp.bfloat16)
    return jnp.einsum("ngf,gfd->ngd", hidden_rows, down_w, preferred_element_type=jnp.float32)


def on_device(keys, values, queries, next_queries, rates, tile_counts, w_gate, w_up, w_down):
    tok_rows = keys.shape[0]
    heads_here = w_gate.shape[0]
    head_dim = w_gate.shape[1]
    tile_total = tok_rows // TILE
    key_tiles = keys.reshape(tile_total, TILE, heads_here, head_dim)
    value_tiles = values.reshape(tile_total, TILE, heads_here, head_dim)
    rate_tiles = rates.reshape(tile_total, TILE, heads_here)
    own_load = tile_counts[0]
    step_scale = float(tok_rows * lax.axis_size("tok")) ** (-0.5)
    query_heads = queries.reshape(tok_rows, heads_here, head_dim)
    next_heads = next_queries.reshape(tok_rows, heads_here, head_dim)
    gradients = tile_grads(key_tiles, value_tiles, rate_tiles, own_load, w_gate, w_up, w_down)
    gate_new, up_new, down_new = new_weights(gradients, w_gate, w_up, w_down, step_scale)
    block_all = forward_rows(query_heads, gate_new, up_new, down_new).reshape(
        tok_rows, heads_here * head_dim
    )
    next_all = forward_rows(next_heads, gate_new, up_new, down_new).reshape(
        tok_rows, heads_here * head_dim
    )
    summed = (
        lax.psum_scatter(block_all, "rep", scatter_dimension=1, tiled=True),
        lax.psum_scatter(next_all, "rep", scatter_dimension=1, tiled=True),
    )
    return (summed[0].astype(jnp.bfloat16), summed[1].astype(jnp.bfloat16))


def solution(mesh):
    return jax.shard_map(
        on_device,
        mesh=mesh,
        in_specs=(
            P(("parts", "tok"), "head"),
            P(("parts", "tok"), "head"),
            P(("parts", "tok"), "head"),
            P(("parts", "tok"), "head"),
            P(("parts", "tok"), "head"),
            P(("parts", "tok")),
            P("head", None, "rep"),
            P("head", None, "rep"),
            P("head", "rep", None),
        ),
        out_specs=(P(("parts", "tok"), ("head", "rep")), P(("parts", "tok"), ("head", "rep"))),
        check_vma=False,
    )
```

profile of v0, /device:TPU:0, one launch (start us, length us, event | category | flops | bytes accessed | tf_op | source)
XLA Modules:
  0.0 504.4 jit_solution(16470410363317762695)
XLA Ops:
  7.2 11.2 %reshape.68 = bf16[12,128,4,512]{3,2,1,0:T(4,128)(2,1)} reshape(bf16[1536,2048]{1,0:T(8,128)(2,1)} %param.11) | data formatting | bytes 12582912 | tf_op jit(solution)/shard_map/reshape | solution.py:74
  18.4 11.2 %reshape.70 = bf16[12,128,4,512]{3,2,1,0:T(4,128)(2,1)} reshape(bf16[1536,2048]{1,0:T(8,128)(2,1)} %param.12) | data formatting | bytes 12582912 | tf_op jit(solution)/shard_map/reshape | solution.py:75
  29.5 1.5 broadcast.28.clone
  31.0 1.6 broadcast_in_dim.3
  32.8 11.4 %while.14 = (s32[]{:T(128)}, f32[4,512,256]{2,1,0:T(8,128)S(1)}, f32[4,512,256]{2,1,0:T(8,128)}, f32[4,256,512]{2,1,0:T(8,128)}, s32[]{:T(128)}, /*index=5*/bf16...) while((s32[]{:T(128)}, f32[4,512,256]{2,1,0:T(8,128)S(1)}, ...), condition=%wide.region_1.2_spmd, body=%wide.region_0.1_spmd.sunk | while | flops 810025472 | bytes 68164952 | solution.py:42
  33.5 0.8 bitcast_convert_fusion.2
  34.2 1.6 constant_dynamic-slice_fusion.3
  36.1 0.5 fusion.46
  37.4 0.5 copy-done.1
  37.8 0.9 convolution_add_fusion.8
  38.8 0.9 convolution_add_fusion.6
  40.1 1.0 copy-done.3
  41.1 1.1 convolution_add_fusion.7
  42.2 1.3 copy-done.4
  44.1 1.3 copy-done
  45.7 8.6 %copy.52 = bf16[1536,2048]{0,1:T(8,128)(2,1)} copy(bf16[1536,2048]{1,0:T(8,128)(2,1)} %param.13) | data formatting | bytes 12582912 | tf_op jit(solution)/shard_map/reshape | solution.py:79
  54.4 333.3 %all-reduce.3.cloned.1.call-done = (f32[4,256,512]{2,1,0:T(8,128)}, f32[4,512,256]{2,1,0:T(8,128)}, f32[4,512,256]{2,1,0:T(8,128)}) async-done(((f32[4,256,512]{2,1,0:T(8,128)}, f32[4,512,256]{2,1,0:T(8,128)}, f32[4,512,256]{2,1,0:T(8,128)}), (f32[4,256,512]{2,1,0:T(8,128)}, f32[4,512,256]{2,1,0:T(8,128)}, f32[4,512,256]{2,1,0:T(8,128)})) %all-reduce.3.cloned.1.call-update) | async-done | bytes 6291472 | tf_op jit(solution)/shard_map/psum | solution.py:54
  387.7 2.3 fusion.19
  390.0 2.1 multiply_convert_fusion.8
  392.2 0.7 copy-done.10
  392.9 1.0 fusion.20
  395.0 0.9 slice-done.1
  396.0 4.5 fusion.24
  400.4 13.3 %fusion.17 = f32[4,512,1536]{2,1,0:T(8,128)} fusion(bf16[4,256,512]{2,1,0:T(8,128)(2,1)S(1)} %multiply_convert_fusion.8, f32[4,256,1536]{2,1,0:T(8,128)} %fusion.24, bf16[4,512,256]{2,1,0:T(8,128)(2,1)S(1)} %multiply_convert_fusion.6, bf16[1536,4,512]{0,2,1:T(8,128)(2,1)} %bitcast.112), kind=kOutput, calls=%fused_computation.36 | convolution fusion | flops 3230662656 | bytes 27262976 | tf_op jit(solution)/shard_map/ngf,gfd->ngd/dot_general | solution.py:66
  413.7 12.7 %copy.33 = f32[1536,2048]{1,0:T(8,128)} copy(f32[1536,2048]{0,1:T(8,128)} %bitcast.119) | data formatting | bytes 25165824 | tf_op jit(solution)/shard_map/reshape | solution.py:83
  426.7 8.8 %copy.53 = bf16[1536,2048]{0,1:T(8,128)(2,1)} copy(bf16[1536,2048]{1,0:T(8,128)(2,1)} %param.14) | data formatting | bytes 12582912 | tf_op jit(solution)/shard_map/reshape | solution.py:80
  435.5 9.2 %fusion.25 = f32[4,256,1536]{2,1,0:T(8,128)} fusion(bf16[4,512,256]{2,1,0:T(8,128)(2,1)S(1)} %multiply_convert_fusion.7, bf16[1536,4,512]{0,2,1:T(8,128)(2,1)} %bitcast.116), kind=kOutput, calls=%fused_computation.59 | convolution fusion | flops 1610612736 | bytes 13631488 | tf_op jit(solution)/shard_map/ngd,gdf->ngf/dot_general | solution.py:63
  444.8 13.7 %fusion.18 = f32[4,512,1536]{2,1,0:T(8,128)} fusion(bf16[4,256,512]{2,1,0:T(8,128)(2,1)S(1)} %multiply_convert_fusion.8, f32[4,256,1536]{2,1,0:T(8,128)} %fusion.25, bf16[4,512,256]{2,1,0:T(8,128)(2,1)S(1)} %multiply_convert_fusion.6, bf16[1536,4,512]{0,2,1:T(8,128)(2,1)} %bitcast.117), kind=kOutput, calls=%fused_computation.37 | convolution fusion | flops 3230662656 | bytes 27262976 | tf_op jit(solution)/shard_map/ngf,gfd->ngd/dot_general | solution.py:66
  458.5 12.7 %copy.38 = f32[1536,2048]{1,0:T(8,128)} copy(f32[1536,2048]{0,1:T(8,128)} %bitcast.118) | data formatting | bytes 25165824 | tf_op jit(solution)/shard_map/reshape | solution.py:86
  471.3 4.9 convert_element_type.56
  476.2 16.7 %reduce-scatter.5.cloned.1.call-done = f32[1536,1024]{1,0:T(8,128)} async-done(((f32[1536,2048]{1,0:T(8,128)}), f32[1536,1024]{1,0:T(8,128)}) %reduce-scatter.5.cloned.1.call-update) | async-done | bytes 6291472 | tf_op jit(solution)/shard_map/reduce_scatter | solution.py:91
  493.0 4.9 convert_element_type.58
  (38 shorter events, 3.4 us)
Async XLA Ops:
  7.2 380.5 %all-reduce.3.cloned.1.call-start = ((), (), s32[]{:S(2)}) async-start(), calls=%async_computation.4 | async-start | bytes 12582912 | tf_op jit(solution)/shard_map/psum | solution.py:54
  31.0 1.7 copy-start.5
  33.4 2.4 copy-start.6
  35.8 1.2 copy-start.8
  36.1 1.7 copy-start.1
  38.7 1.3 copy-start.2
  38.7 2.4 copy-start.3
  42.2 1.3 copy-start.4
  44.1 1.3 copy-start
  45.5 425.8 %reduce-scatter.3.cloned.1.call-start = ((), (), s32[]{:S(2)}) async-start(), calls=%async_computation.2 | async-start | bytes 18874368 | tf_op jit(solution)/shard_map/reduce_scatter | solution.py:90
  387.7 4.4 copy-start.11
  390.0 2.1 copy-start.7
  390.0 2.2 copy-start.9
  390.0 2.8 copy-start.10
  392.9 2.2 slice-start
  393.9 2.1 slice-start.1
  426.5 66.5 %reduce-scatter.5.cloned.1.call-start = ((), (), s32[]{:S(2)}) async-start(), calls=%async_computation.3 | async-start | bytes 18874368 | tf_op jit(solution)/shard_map/reduce_scatter | solution.py:91
Sparse Core Ops, SparseCore 0:
  45.6 341.9 all-reduce.2
  426.6 20.4 reduce-scatter.2
  471.4 21.5 reduce-scatter.4
where the time goes:
time: 508 us; the launch traced here: 504 us
  waiting for transfers between devices  350 us (69%)
  local copies, waits for them, and re-layouts  77 us (15%)
  matrix products  44.7 us (9%)
  other arithmetic  16.8 us (3%)
  between operations  13.9 us (3%)
    psum x1, waiting for transfers between devices, new_weights(): summed = lax.psum((gradients[0], gradients[1], gradients[2]), 'tok')  333 us
    dot_general x2, matrix products, forward_rows(): jnp.einsum('ngf,gfd->ngd', hidden_rows, down_w, preferred_element_type=jn...  27 us
    reduce_scatter x1, waiting for transfers between devices, on_device(): lax.psum_scatter(next_all, 'rep', scatter_dimension=1, tiled=True)  16.7 us
    dot_general x2, matrix products, forward_rows(): jnp.einsum('ngd,gdf->ngf', query_rows, gate_w, preferred_element_type=jnp...  13.7 us
    reshape x1, local copies, waits for them, and re-layouts, on_device(): forward_rows(query_heads, gate_new, up_new, down_new)  12.7 us
    reshape x1, local copies, waits for them, and re-layouts, on_device(): forward_rows(next_heads, gate_new, up_new, down_new)  12.7 us
    reshape x1, local copies, waits for them, and re-layouts, on_device(): value_tiles = values.reshape(tile_total, TILE, heads_here, head_dim)  11.2 us
    reshape x1, local copies, waits for them, and re-layouts, on_device(): key_tiles = keys.reshape(tile_total, TILE, heads_here, head_dim)  11.2 us
  transfers between devices with their start and end apart: 3, of which 2 were waited for; matrix products, arithmetic and copies ran while one was open for 12% of the time, Pallas kernels for 0%

commit v1 on v0

v1 whole, which is shorter than its diff:
```python
import functools

import jax
import jax.numpy as jnp
from jax import lax
from jax.experimental import pallas as pl
from jax.experimental.pallas import tpu as pltpu
from jax.sharding import PartitionSpec as P

TILE = 128
ROWS = 512
F32 = jnp.float32
BF16 = jnp.bfloat16
MESH = pl.DeviceIdType.MESH


def dot(a, b, ca, cb):
    return lax.dot_general(a, b, (((ca,), (cb,)), ((), ())), preferred_element_type=F32)


def kernel(
    n, hpc, scale,
    count_ref, rates_ref, k_hbm, v_hbm, q_hbm, qn_hbm, wg_hbm, wu_hbm, wd_hbm,
    out_hbm, next_hbm,
    kv, xs, w_gu, w_d, g_gu, g_d, s_gu, s_d, o_gu, o_d, m_gu, m_d, n_gu, n_d, y_acc, stage,
    kv_sem, x_sem, w_sem, ex_send, ex_recv, s_send, o_recv, m_recv, n_send, n_recv, out_sem,
):
    pos = lax.axis_index("tok")
    rep = lax.axis_index("rep")
    half_n = n // 2
    is_left = pos < half_n
    is_mid = jnp.logical_or(pos == half_n - 1, pos == half_n)
    is_end = jnp.logical_or(pos == 0, pos == n - 1)
    inward = jnp.where(is_left, pos + 1, pos - 1)
    outward = jnp.where(is_left, pos - 1, pos + 1)
    not_end = jnp.logical_not(is_end)
    not_mid = jnp.logical_not(is_mid)
    tok_rows, dh = xs.shape[2], xs.shape[3]
    units = 2 * hpc
    pieces = 3 * units
    chunks = tok_rows // ROWS

    first = rep * hpc
    w_pairs = lambda j: ((wg_hbm, w_gu.at[j, 0]), (wu_hbm, w_gu.at[j, 1]), (wd_hbm, w_d.at[j]))
    own_w = []
    kv_in = []
    x_in = []
    for j in range(hpc):
        cols = pl.ds(pl.multiple_of((first + j) * dh, dh), dh)
        own_w.append([
            pltpu.make_async_copy(src.at[first + j], dst, w_sem.at[j, t])
            for t, (src, dst) in enumerate(w_pairs(2 * j))
        ])
        kv_in.append([
            pltpu.make_async_copy(src.at[:, cols], kv.at[j, t], kv_sem.at[j, t])
            for t, src in enumerate((k_hbm, v_hbm))
        ])
        x_in.append([
            pltpu.make_async_copy(src.at[:, cols], xs.at[j, t], x_sem.at[j, t])
            for t, src in enumerate((q_hbm, qn_hbm))
        ])
        for c in own_w[j] + kv_in[j]:
            c.start()

    barrier = pltpu.get_barrier_semaphore()
    pl.semaphore_signal(barrier, inc=1, device_id={"tok": inward}, device_id_type=MESH)
    pl.semaphore_signal(barrier, inc=1, device_id={"rep": 1 - rep}, device_id_type=MESH)

    @pl.when(not_end)
    def _():
        pl.semaphore_signal(barrier, inc=1, device_id={"tok": outward}, device_id_type=MESH)
        pl.semaphore_wait(barrier, 3)

    @pl.when(is_end)
    def _():
        pl.semaphore_wait(barrier, 2)

    exchange = []
    for j in range(hpc):
        theirs = (1 - rep) * hpc + j
        exchange.append([
            pltpu.make_async_remote_copy(
                src_ref=src.at[theirs], dst_ref=dst, send_sem=ex_send.at[j, t],
                recv_sem=ex_recv.at[j, t], device_id={"rep": 1 - rep}, device_id_type=MESH,
            )
            for t, (src, dst) in enumerate(w_pairs(2 * j + 1))
        ])
        for c in exchange[j]:
            c.start()
    for j in range(hpc):
        for c in x_in[j]:
            c.start()

    def piece(pair, p):
        u, t = divmod(p, 3)
        return pair[1].at[u] if t == 2 else pair[0].at[u, t]

    W, G, S, O, M, N = (w_gu, w_d), (g_gu, g_d), (s_gu, s_d), (o_gu, o_d), (m_gu, m_d), (n_gu, n_d)

    def send_in(p, to, recv):
        return pltpu.make_async_remote_copy(
            src_ref=piece(S, p), dst_ref=piece(to, p), send_sem=s_send.at[p], recv_sem=recv.at[p],
            device_id={"tok": inward}, device_id_type=MESH,
        )

    def send_out(p):
        return pltpu.make_async_remote_copy(
            src_ref=piece(N, p), dst_ref=piece(N, p), send_sem=n_send.at[p], recv_sem=n_recv.at[p],
            device_id={"tok": outward}, device_id_type=MESH,
        )

    def grads(u):
        j, half = divmod(u, 2)
        if half == 0:
            for c in kv_in[j] + own_w[j]:
                c.wait()
        else:
            for c in exchange[j]:
                c.wait_recv()
        g_gu[u] = jnp.zeros_like(g_gu[u])
        g_d[u] = jnp.zeros_like(g_d[u])
        limit = count_ref[0] * TILE

        @pl.loop(0, chunks)
        def _(c):
            start = pl.multiple_of(c * ROWS, ROWS)
            rows = pl.ds(start, ROWS)
            key = kv[j, 0, rows, :]
            value = kv[j, 1, rows, :]
            rate = rates_ref[rows, :].astype(F32)
            eta = jnp.where(rep == 0, rate[:, j:j + 1], rate[:, hpc + j:hpc + j + 1])
            at = start + lax.broadcasted_iota(jnp.int32, (ROWS, 1), 0)
            eta = jnp.where(at < limit, eta, 0.0)
            a = dot(key, w_gu[u, 0], 1, 0)
            b = dot(key, w_gu[u, 1], 1, 0)
            e = dot(value, w_d[u], 1, 1)
            sig = jax.nn.sigmoid(a)
            silu = a * sig
            hid = (eta * silu * b).astype(BF16)
            back = eta * e
            r_gate = (back * b * (sig * (1.0 + a * (1.0 - sig)))).astype(BF16)
            r_up = (back * silu).astype(BF16)
            both = dot(key, jnp.concatenate([r_gate, r_up], axis=1), 0, 0)
            fh = r_gate.shape[1]
            g_gu[u, 0] += both[:, :fh]
            g_gu[u, 1] += both[:, fh:]
            g_d[u] += dot(hid, value, 0, 0)

        @pl.when(is_end)
        def _():
            for p in range(3 * u, 3 * u + 3):
                piece(S, p)[...] = piece(G, p)[...].astype(BF16)
                send_in(p, O, o_recv).start()

    def join(p):
        send_in(p, O, o_recv).wait_recv()
        piece(S, p)[...] = (piece(G, p)[...] + piece(O, p)[...].astype(F32)).astype(BF16)

        @pl.when(is_mid)
        def _():
            send_in(p, M, m_recv).start()

        @pl.when(not_mid)
        def _():
            send_in(p, O, o_recv).start()

    def finish(p):
        @pl.when(is_mid)
        def _():
            send_in(p, M, m_recv).wait_recv()
            axis = 1 if p % 3 == 2 else 0
            old = piece(W, p)[...].astype(F32)
            total = piece(S, p)[...].astype(F32) + piece(M, p)[...].astype(F32)
            new = old + scale * total
            target = jnp.sqrt(jnp.sum(old * old, axis=axis, keepdims=True))
            current = jnp.sqrt(jnp.sum(new * new, axis=axis, keepdims=True) + 1e-06)
            piece(N, p)[...] = (new * (target / current)).astype(BF16)

        @pl.when(not_mid)
        def _():
            send_out(p).wait_recv()

        send_out(p).start()

    out_copies = []

    def forward(u):
        j, half = divmod(u, 2)
        if half == 0:
            for c in x_in[j]:
                c.wait()

        for t, dst in enumerate((out_hbm, next_hbm)):
            @pl.loop(0, chunks)
            def _(c):
                rows = pl.ds(pl.multiple_of(c * ROWS, ROWS), ROWS)
                x = xs[j, t, rows, :]
                a = dot(x, n_gu[u, 0], 1, 0)
                b = dot(x, n_gu[u, 1], 1, 0)
                hid = (a * jax.nn.sigmoid(a) * b).astype(BF16)
                y = dot(hid, n_d[u], 1, 0)
                if half == 0:
                    y_acc[t, rows, :] = y
                else:
                    stage[j, t, rows, :] = (y_acc[t, rows, :] + y).astype(BF16)
            if half == 1:
                copy = pltpu.make_async_copy(
                    stage.at[j, t], dst.at[:, pl.ds(j * dh, dh)], out_sem.at[j, t]
                )
                copy.start()
                out_copies.append(copy)

    grads(0)
    for k in range(pieces + 1):
        if k + 1 < units:
            grads(k + 1)

        @pl.when(not_end)
        def _():
            if k < pieces:
                join(k)
            if k >= 1:
                finish(k - 1)

        if k >= 3 and k % 3 == 0:
            u = k // 3 - 1

            @pl.when(is_end)
            def _():
                for p in range(3 * u, 3 * u + 3):
                    send_out(p).wait_recv()

            forward(u)

    for p in range(pieces):
        send_in(p, O, o_recv).wait_send()

    @pl.when(not_end)
    def _():
        for p in range(pieces):
            send_out(p).wait_send()

    for j in range(hpc):
        for c in exchange[j]:
            c.wait_send()
    for c in out_copies:
        c.wait()


def on_device(n, reps, keys, values, queries, next_queries, rates, tile_counts, w_gate, w_up, w_down):
    tok_rows = keys.shape[0]
    heads_here, dh, fh = w_gate.shape
    hpc = heads_here // reps
    units = 2 * hpc
    pieces = 3 * units
    scale = float(tok_rows * n) ** (-0.5)
    gu = (units, 2, dh, fh)
    down = (units, fh, dh)
    out = jax.ShapeDtypeStruct((tok_rows, hpc * dh), BF16)
    hbm = pl.BlockSpec(memory_space=pl.ANY)
    dma = pltpu.SemaphoreType.DMA
    pair = lambda dtype: [pltpu.VMEM(gu, dtype), pltpu.VMEM(down, dtype)]
    return pl.pallas_call(
        functools.partial(kernel, n, hpc, scale),
        out_shape=(out, out),
        in_specs=[
            pl.BlockSpec(memory_space=pltpu.SMEM),
            pl.BlockSpec(memory_space=pltpu.VMEM),
        ] + [hbm] * 7,
        out_specs=(hbm, hbm),
        scratch_shapes=[
            pltpu.VMEM((hpc, 2, tok_rows, dh), BF16),
            pltpu.VMEM((hpc, 2, tok_rows, dh), BF16),
            *pair(BF16), *pair(F32), *pair(BF16), *pair(BF16), *pair(BF16), *pair(BF16),
            pltpu.VMEM((2, tok_rows, dh), F32),
            pltpu.VMEM((hpc, 2, tok_rows, dh), BF16),
            dma((hpc, 2)), dma((hpc, 2)), dma((hpc, 3)), dma((hpc, 3)), dma((hpc, 3)),
            dma((pieces,)), dma((pieces,)), dma((pieces,)), dma((pieces,)), dma((pieces,)),
            dma((hpc, 2)),
        ],
        compiler_params=pltpu.CompilerParams(
            collective_id=0, has_side_effects=True, vmem_limit_bytes=60 * 2**20
        ),
    )(tile_counts, rates, keys, values, queries, next_queries, w_gate, w_up, w_down)


def solution(mesh):
    rows = P(("parts", "tok"), "head")
    outs = P(("parts", "tok"), ("head", "rep"))
    return jax.shard_map(
        functools.partial(on_device, mesh.shape["tok"], mesh.shape["rep"]),
        mesh=mesh,
        in_specs=(
            rows, rows, rows, rows, rows,
            P(("parts", "tok")),
            P("head", None, "rep"),
            P("head", None, "rep"),
            P("head", "rep", None),
        ),
        out_specs=(outs, outs),
        check_vma=False,
    )
```

time: 508 us -> 107 us (0.21)
  waiting for transfers between devices: 350 us -> 0 us
  Pallas kernels: 0 us -> 98.4 us
  local copies, waits for them, and re-layouts: 77 us -> 7.36 us
  matrix products: 44.7 us -> 0 us
  other arithmetic: 16.8 us -> 0 us
  between operations: 13.9 us -> 1.29 us
    psum x1 -> x0, waiting for transfers between devices: 333 us -> none  [new_weights(): summed = lax.psum((gradients[0], gradients[1], gradients[2]), 'tok')]
    pallas_call x0 -> x1, Pallas kernels: none -> 98.4 us  [on_device(): pl.pallas_call(functools.partial(kernel, n, hpc, scale), out_shape=(out,...]
    reshape x6 -> x0, local copies, waits for them, and re-layouts: 65.2 us -> none  [the longest x1 12.7 us: on_device(): forward_rows(query_heads, gate_new, up_new, down_new)]
    dot_general x10 -> x0, matrix products: 44.7 us -> none  [the longest x2 27 us: forward_rows(): jnp.einsum('ngf,gfd->ngd', hidden_rows, down_w, preferred_element_type=jn...]
    reduce_scatter x2 -> x0, waiting for transfers between devices: 16.7 us -> none  [the longest x1 16.7 us: on_device(): lax.psum_scatter(next_all, 'rep', scatter_dimension=1, tiled=True)]
    convert_element_type x6 -> x0, other arithmetic: 13.5 us -> none  [the longest x2 9.9 us: on_device(): return (summed[0].astype(jnp.bfloat16), summed[1].astype(jnp.bfloat16))]
  transfers between devices with their start and end apart: 3 -> 0, of which waited for: 2 -> 0; matrix products, arithmetic and copies ran while one was open for 12% -> 0% of each run, Pallas kernels for 0% -> 0%
where the time goes in v1:
time: 107 us
  Pallas kernels  98.4 us (92%)
  local copies, waits for them, and re-layouts  7.36 us (7%)
  between operations  1.29 us (1%)
    pallas_call x1, Pallas kernels, on_device(): pl.pallas_call(functools.partial(kernel, n, hpc, scale), out_shape=(out,...  98.4 us
    unnamed x5, local copies, waits for them, and re-layouts  7.36 us

profile of v1, /device:TPU:0, one launch (start us, length us, event | category | flops | bytes accessed | tf_op | source)
XLA Modules:
  0.0 107.0 jit_solution(9279440207911756675)
XLA Ops:
  1.3 1.7 %copy.11.rates_ref = bf16[1536,4]{1,0:T(8,128)(2,1)} copy(bf16[1536,4]{0,1:T(4,128)(2,1)} %param.13) | data formatting | bytes 24576 | tf_op args[4]
  2.9 98.4 %shard_map.104 = (bf16[1536,1024]{1,0:T(8,128)(2,1)}, bf16[1536,1024]{1,0:T(8,128)(2,1)}) custom-call(s32[1]{0:T(128)S(6)} %copy.14.count_ref, bf16[1536,4]{1,0:T(8,128)(2,1)} %copy.11.rates_ref, bf16[1536,2048]{1,0:T(8,128)(2,1)} %k_hbm.1, bf16[1536,2048]{1,0:T(8,128)(2,1)} %v_hbm.1, bf16[1536,2048]{1,0:T(8,128)(2,1)} %q_hbm.1, bf16[1536,2048]{1,0:T(8,128)(2,1)} %qn_hbm.1, ...), custom_call_target="tpu_custom_call" | custom-call | tf_op jit(solution)/shard_map/pallas_call | solution.py:263
  101.3 0.0 copy-start
  101.3 4.0 %copy.15 = bf16[1536,1024]{1,0:T(8,128)(2,1)} copy(bf16[1536,1024]{1,0:T(8,128)(2,1)} %get-tuple-element.4) | data formatting | bytes 6291456
  105.4 0.0 copy-done
  105.4 1.7 %copy.16 = bf16[1536,1024]{1,0:T(8,128)(2,1)} copy(bf16[1536,1024]{1,0:T(8,128)(2,1)S(1)} %copy-done) | data formatting | bytes 6291456
Async XLA Ops:
  101.3 4.0 %copy-start = (bf16[1536,1024]{1,0:T(8,128)(2,1)S(1)}, bf16[1536,1024]{1,0:T(8,128)(2,1)}, u32[]{:S(2)}) copy-start(bf16[1536,1024]{1,0:T(8,128)(2,1)} %get-tuple-element.5) | copy-start | bytes 9437188

commit v2 on v1

v2 whole, which is shorter than its diff:
```python
import functools

import jax
import jax.numpy as jnp
from jax import lax
from jax.experimental import pallas as pl
from jax.experimental.pallas import tpu as pltpu
from jax.sharding import PartitionSpec as P

TILE = 128
ROWS = 512
SUBS = 2
F32 = jnp.float32
BF16 = jnp.bfloat16
MESH = pl.DeviceIdType.MESH


def dot(a, b, ca, cb):
    return lax.dot_general(a, b, (((ca,), (cb,)), ((), ())), preferred_element_type=F32)


def kernel(
    n, hpc, scale,
    count_ref, rates_ref, k_hbm, v_hbm, q_hbm, qn_hbm, wg_hbm, wu_hbm, wd_hbm,
    out_hbm, next_hbm,
    kv, xs, w_gu, w_d, g_gu, g_d, s_gu, s_d, o_gu, o_d, m_gu, m_d, n_gu, n_d, y_acc, hids, stage,
    kv_sem, x_sem, w_sem, ex_send, ex_recv, s_send, o_recv, m_recv, n_send, n_recv, out_sem,
):
    pos = lax.axis_index("tok")
    rep = lax.axis_index("rep")
    half_n = n // 2
    is_left = pos < half_n
    is_mid = jnp.logical_or(pos == half_n - 1, pos == half_n)
    is_end = jnp.logical_or(pos == 0, pos == n - 1)
    inward = jnp.where(is_left, pos + 1, pos - 1)
    outward = jnp.where(is_left, pos - 1, pos + 1)
    not_end = jnp.logical_not(is_end)
    not_mid = jnp.logical_not(is_mid)
    tok_rows, dh = xs.shape[2], xs.shape[3]
    units = 2 * hpc
    pieces = 3 * SUBS * units
    chunks = tok_rows // ROWS

    first = rep * hpc
    w_pairs = lambda j: ((wg_hbm, w_gu.at[j, 0]), (wu_hbm, w_gu.at[j, 1]), (wd_hbm, w_d.at[j]))
    own_w = []
    kv_in = []
    x_in = []
    for j in range(hpc):
        cols = pl.ds(pl.multiple_of((first + j) * dh, dh), dh)
        own_w.append([
            pltpu.make_async_copy(src.at[first + j], dst, w_sem.at[j, t])
            for t, (src, dst) in enumerate(w_pairs(2 * j))
        ])
        kv_in.append([
            pltpu.make_async_copy(src.at[:, cols], kv.at[j, t], kv_sem.at[j, t])
            for t, src in enumerate((k_hbm, v_hbm))
        ])
        x_in.append([
            pltpu.make_async_copy(src.at[:, cols], xs.at[j, t], x_sem.at[j, t])
            for t, src in enumerate((q_hbm, qn_hbm))
        ])
        for c in own_w[j] + kv_in[j]:
            c.start()

    barrier = pltpu.get_barrier_semaphore()
    pl.semaphore_signal(barrier, inc=1, device_id={"tok": inward}, device_id_type=MESH)
    pl.semaphore_signal(barrier, inc=1, device_id={"rep": 1 - rep}, device_id_type=MESH)

    @pl.when(not_end)
    def _():
        pl.semaphore_signal(barrier, inc=1, device_id={"tok": outward}, device_id_type=MESH)
        pl.semaphore_wait(barrier, 3)

    @pl.when(is_end)
    def _():
        pl.semaphore_wait(barrier, 2)

    exchange = []
    for j in range(hpc):
        theirs = (1 - rep) * hpc + j
        exchange.append([
            pltpu.make_async_remote_copy(
                src_ref=src.at[theirs], dst_ref=dst, send_sem=ex_send.at[j, t],
                recv_sem=ex_recv.at[j, t], device_id={"rep": 1 - rep}, device_id_type=MESH,
            )
            for t, (src, dst) in enumerate(w_pairs(2 * j + 1))
        ])
        for c in exchange[j]:
            c.start()
    for j in range(hpc):
        for c in x_in[j]:
            c.start()

    W, G, S, O, M, N = (w_gu, w_d), (g_gu, g_d), (s_gu, s_d), (o_gu, o_d), (m_gu, m_d), (n_gu, n_d)
    fh = w_gu.shape[3]
    width = fh // SUBS
    order = []
    for u in range(units):
        if u == units - 1:
            order += [(u, t, s) for s in range(SUBS) for t in range(2)] + [(u, 2, s) for s in range(SUBS)]
        else:
            order += [(u, t, s) for s in range(SUBS) for t in range(3)]

    def piece(pair, p):
        u, t, s = order[p]
        return pair[1].at[u, s] if t == 2 else pair[0].at[u, t, s]

    def window(pair, p):
        u, t, s = order[p]
        part = pl.ds(s * width, width)
        return pair[1].at[u, part, :] if t == 2 else pair[0].at[u, t, :, part]

    def send_in(p, to, recv):
        return pltpu.make_async_remote_copy(
            src_ref=piece(S, p), dst_ref=piece(to, p), send_sem=s_send.at[p], recv_sem=recv.at[p],
            device_id={"tok": inward}, device_id_type=MESH,
        )

    def send_out(p):
        return pltpu.make_async_remote_copy(
            src_ref=piece(N, p), dst_ref=piece(N, p), send_sem=n_send.at[p], recv_sem=n_recv.at[p],
            device_id={"tok": outward}, device_id_type=MESH,
        )

    limit = count_ref[0] * TILE

    def grad_chunk(u, lo, wide, start, fresh):
        j = u // 2
        rows = pl.ds(start, ROWS)
        part = slice(lo, lo + wide)
        key = kv[j, 0, rows, :]
        value = kv[j, 1, rows, :]
        rate = rates_ref[:, rows].astype(F32)
        eta = jnp.where(rep == 0, rate[j:j + 1, :], rate[hpc + j:hpc + j + 1, :])
        at = start + lax.broadcasted_iota(jnp.int32, (1, ROWS), 1)
        eta = jnp.where(at < limit, eta, 0.0)
        eta = jnp.transpose(jnp.broadcast_to(eta, (8, ROWS)))[:, :1]
        a = dot(key, w_gu[u, 0, :, part], 1, 0)
        b = dot(key, w_gu[u, 1, :, part], 1, 0)
        e = dot(value, w_d[u, part, :], 1, 1)
        sig = jax.nn.sigmoid(a)
        silu = a * sig
        hid = (eta * silu * b).astype(BF16)
        back = eta * e
        r_gate = (back * b * (sig * (1.0 + a * (1.0 - sig)))).astype(BF16)
        r_up = (back * silu).astype(BF16)
        both = dot(key, jnp.concatenate([r_gate, r_up], axis=1), 0, 0)
        down = dot(hid, value, 0, 0)
        if fresh:
            g_gu[u, 0, :, part] = both[:, :wide]
            g_gu[u, 1, :, part] = both[:, wide:]
            g_d[u, part, :] = down
        else:
            g_gu[u, 0, :, part] += both[:, :wide]
            g_gu[u, 1, :, part] += both[:, wide:]
            g_d[u, part, :] += down

    def send_first(u, subs):
        @pl.when(is_end)
        def _():
            for p, (pu, _t, ps) in enumerate(order):
                if pu == u and ps in subs:
                    piece(S, p)[...] = window(G, p)[...].astype(BF16)
                    send_in(p, O, o_recv).start()

    def grads_sub(u, s):
        lo = s * width
        grad_chunk(u, lo, width, 0, True)

        @pl.loop(1, chunks)
        def _(c):
            grad_chunk(u, lo, width, pl.multiple_of(c * ROWS, ROWS), False)

        send_first(u, (s,))

    def grads_step(u, c):
        j, half = divmod(u, 2)
        if c == 0:
            for w in (exchange[j] if half else kv_in[j] + own_w[j]):
                w.wait_recv() if half else w.wait()
        grad_chunk(u, 0, fh, c * ROWS, c == 0)
        if c == chunks - 1:
            send_first(u, tuple(range(SUBS)))

    def join(p):
        send_in(p, O, o_recv).wait_recv()
        total = window(G, p)[...] + piece(O, p)[...].astype(F32)
        piece(S, p)[...] = total.astype(BF16)

        @pl.when(is_mid)
        def _():
            send_in(p, M, m_recv).start()

        @pl.when(not_mid)
        def _():
            send_in(p, O, o_recv).start()

        window(G, p)[...] = total

    def finish(p):
        @pl.when(is_mid)
        def _():
            axis = 1 if order[p][1] == 2 else 0
            old = window(W, p)[...].astype(F32)
            send_in(p, M, m_recv).wait_recv()
            new = old + scale * (window(G, p)[...] + piece(M, p)[...].astype(F32))
            target = jnp.sqrt(jnp.sum(old * old, axis=axis, keepdims=True))
            current = jnp.sqrt(jnp.sum(new * new, axis=axis, keepdims=True) + 1e-06)
            piece(N, p)[...] = (new * (target / current)).astype(BF16)

        @pl.when(not_mid)
        def _():
            send_out(p).wait_recv()

        send_out(p).start()

    def arrived(u, ts):
        @pl.when(is_end)
        def _():
            for p, (pu, t, _s) in enumerate(order):
                if pu == u and t in ts:
                    send_out(p).wait_recv()

    def hidden(u, t):
        j = u // 2
        gate = jnp.concatenate([n_gu[u, 0, s] for s in range(SUBS)], axis=1)
        up = jnp.concatenate([n_gu[u, 1, s] for s in range(SUBS)], axis=1)

        @pl.loop(0, chunks)
        def _(c):
            rows = pl.ds(pl.multiple_of(c * ROWS, ROWS), ROWS)
            x = xs[j, t, rows, :]
            a = dot(x, gate, 1, 0)
            b = dot(x, up, 1, 0)
            hids[t, rows, :] = (a * jax.nn.sigmoid(a) * b).astype(BF16)

    def out_copy(j, t, c):
        rows = pl.ds(c * ROWS if isinstance(c, int) else pl.multiple_of(c * ROWS, ROWS), ROWS)
        return pltpu.make_async_copy(
            stage.at[j, t, rows, :], (out_hbm, next_hbm)[t].at[rows, pl.ds(j * dh, dh)], out_sem.at[j, t, c]
        )

    def outputs(u, t):
        j, half = divmod(u, 2)
        down = jnp.concatenate([n_d[u, s] for s in range(SUBS)], axis=0)

        @pl.loop(0, chunks)
        def _(c):
            rows = pl.ds(pl.multiple_of(c * ROWS, ROWS), ROWS)
            y = dot(hids[t, rows, :], down, 1, 0)
            if half == 0:
                y_acc[t, rows, :] = y
            else:
                stage[j, t, rows, :] = (y_acc[t, rows, :] + y).astype(BF16)
                out_copy(j, t, c).start()

    def forward_step(u, t):
        j, half = divmod(u, 2)
        if half == 0:
            x_in[j][t].wait()
        if t == 0:
            arrived(u, (0, 1, 2))
        hidden(u, t)
        outputs(u, t)

    steps = {0: lambda: grads_sub(0, 1)}
    at = 1
    for u in range(1, units):
        for c in range(chunks):
            steps[at] = functools.partial(grads_step, u, c)
            at += 1
    per_unit = 3 * SUBS
    for u in range(units - 1):
        at = max(at, per_unit * (u + 1) + 1)
        for t in range(2):
            steps[at] = functools.partial(forward_step, u, t)
            at += 1

    for c in kv_in[0] + own_w[0]:
        c.wait()
    grads_sub(0, 0)
    for k in range(pieces + 1):
        if k in steps:
            steps.pop(k)()

        @pl.when(not_end)
        def _():
            if k < pieces:
                join(k)
            if k >= 1:
                finish(k - 1)

    for k in sorted(steps):
        steps[k]()
    last = units - 1
    arrived(last, (0, 1))
    for t in range(2):
        hidden(last, t)
    arrived(last, (2,))
    for t in range(2):
        outputs(last, t)

    for p in range(pieces):
        send_in(p, O, o_recv).wait_send()

    @pl.when(not_end)
    def _():
        for p in range(pieces):
            send_out(p).wait_send()

    for j in range(hpc):
        for c in exchange[j]:
            c.wait_send()
        for t in range(2):
            for c in range(chunks):
                out_copy(j, t, c).wait()


def on_device(n, reps, keys, values, queries, next_queries, rates, tile_counts, w_gate, w_up, w_down):
    tok_rows = keys.shape[0]
    heads_here, dh, fh = w_gate.shape
    hpc = heads_here // reps
    units = 2 * hpc
    pieces = 3 * SUBS * units
    scale = float(tok_rows * n) ** (-0.5)
    gu = (units, 2, dh, fh)
    down = (units, fh, dh)
    gu_cut = (units, 2, SUBS, dh, fh // SUBS)
    down_cut = (units, SUBS, fh // SUBS, dh)
    out = jax.ShapeDtypeStruct((tok_rows, hpc * dh), BF16)
    hbm = pl.BlockSpec(memory_space=pl.ANY)
    dma = pltpu.SemaphoreType.DMA
    pair = lambda dtype: [pltpu.VMEM(gu, dtype), pltpu.VMEM(down, dtype)]
    cut = lambda: [pltpu.VMEM(gu_cut, BF16), pltpu.VMEM(down_cut, BF16)]
    return pl.pallas_call(
        functools.partial(kernel, n, hpc, scale),
        out_shape=(out, out),
        in_specs=[
            pl.BlockSpec(memory_space=pltpu.SMEM),
            pl.BlockSpec(memory_space=pltpu.VMEM),
        ] + [hbm] * 7,
        out_specs=(hbm, hbm),
        scratch_shapes=[
            pltpu.VMEM((hpc, 2, tok_rows, dh), BF16),
            pltpu.VMEM((hpc, 2, tok_rows, dh), BF16),
            *pair(BF16), *pair(F32), *cut(), *cut(), *cut(), *cut(),
            pltpu.VMEM((2, tok_rows, dh), F32),
            pltpu.VMEM((2, tok_rows, fh), BF16),
            pltpu.VMEM((hpc, 2, tok_rows, dh), BF16),
            dma((hpc, 2)), dma((hpc, 2)), dma((hpc, 3)), dma((hpc, 3)), dma((hpc, 3)),
            dma((pieces,)), dma((pieces,)), dma((pieces,)), dma((pieces,)), dma((pieces,)),
            dma((hpc, 2, tok_rows // ROWS)),
        ],
        compiler_params=pltpu.CompilerParams(
            collective_id=0, has_side_effects=True, vmem_limit_bytes=60 * 2**20
        ),
    )(tile_counts, rates.T, keys, values, queries, next_queries, w_gate, w_up, w_down)


def solution(mesh):
    rows = P(("parts", "tok"), "head")
    outs = P(("parts", "tok"), ("head", "rep"))
    return jax.shard_map(
        functools.partial(on_device, mesh.shape["tok"], mesh.shape["rep"]),
        mesh=mesh,
        in_specs=(
            rows, rows, rows, rows, rows,
            P(("parts", "tok")),
            P("head", None, "rep"),
            P("head", None, "rep"),
            P("head", "rep", None),
        ),
        out_specs=(outs, outs),
        check_vma=False,
    )
```

time: 107 us -> 105 us (0.981)
  local copies, waits for them, and re-layouts: 7.36 us -> 5.69 us
    unnamed x5 -> x4, local copies, waits for them, and re-layouts: 7.36 us -> 5.69 us
where the time goes in v2:
time: 105 us
  Pallas kernels  97.9 us (93%)
  local copies, waits for them, and re-layouts  5.69 us (5%)
  between operations  1.3 us (1%)
    pallas_call x1, Pallas kernels, on_device(): pl.pallas_call(functools.partial(kernel, n, hpc, scale), out_shape=(out,...  97.9 us
    unnamed x4, local copies, waits for them, and re-layouts  5.69 us

profile of v2, /device:TPU:0, one launch (start us, length us, event | category | flops | bytes accessed | tf_op | source)
XLA Modules:
  0.0 104.9 jit_solution(15637786410766884064)
XLA Ops:
  1.3 97.9 %shard_map.104 = (bf16[1536,1024]{1,0:T(8,128)(2,1)}, bf16[1536,1024]{1,0:T(8,128)(2,1)}) custom-call(s32[1]{0:T(128)S(6)} %copy.13.count_ref, bf16[4,1536]{1,0:T(4,128)(2,1)} %bitcast.1, bf16[1536,2048]{1,0:T(8,128)(2,1)} %k_hbm.1, bf16[1536,2048]{1,0:T(8,128)(2,1)} %v_hbm.1, bf16[1536,2048]{1,0:T(8,128)(2,1)} %q_hbm.1, bf16[1536,2048]{1,0:T(8,128)(2,1)} %qn_hbm.1, ...), custom_call_target="tpu_custom_call" | custom-call | tf_op jit(solution)/shard_map/pallas_call | solution.py:336
  99.2 0.0 copy-start
  99.2 4.0 %copy.14 = bf16[1536,1024]{1,0:T(8,128)(2,1)} copy(bf16[1536,1024]{1,0:T(8,128)(2,1)} %get-tuple-element.4) | data formatting | bytes 6291456
  103.2 0.0 copy-done
  103.2 1.7 %copy.15 = bf16[1536,1024]{1,0:T(8,128)(2,1)} copy(bf16[1536,1024]{1,0:T(8,128)(2,1)S(1)} %copy-done) | data formatting | bytes 6291456
Async XLA Ops:
  99.2 4.0 %copy-start = (bf16[1536,1024]{1,0:T(8,128)(2,1)S(1)}, bf16[1536,1024]{1,0:T(8,128)(2,1)}, u32[]{:S(2)}) copy-start(bf16[1536,1024]{1,0:T(8,128)(2,1)} %get-tuple-element.5) | copy-start | bytes 9437188

commit v3 on v2

--- a/solution.py
+++ b/solution.py
@@ -22,9 +22,9 @@
 def kernel(
     n, hpc, scale,
     count_ref, rates_ref, k_hbm, v_hbm, q_hbm, qn_hbm, wg_hbm, wu_hbm, wd_hbm,
-    out_hbm, next_hbm,
-    kv, xs, w_gu, w_d, g_gu, g_d, s_gu, s_d, o_gu, o_d, m_gu, m_d, n_gu, n_d, y_acc, hids, stage,
-    kv_sem, x_sem, w_sem, ex_send, ex_recv, s_send, o_recv, m_recv, n_send, n_recv, out_sem,
+    out_ref, next_ref,
+    kv, xs, w_gu, w_d, g_gu, g_d, s_gu, s_d, o_gu, o_d, m_gu, m_d, n_gu, n_d, y_acc, hids,
+    kv_sem, x_sem, w_sem, ex_send, ex_recv, s_send, o_recv, m_recv, n_send, n_recv,
 ):
     pos = lax.axis_index("tok")
     rep = lax.axis_index("rep")
@@ -235,12 +235,6 @@
             b = dot(x, up, 1, 0)
             hids[t, rows, :] = (a * jax.nn.sigmoid(a) * b).astype(BF16)
 
-    def out_copy(j, t, c):
-        rows = pl.ds(c * ROWS if isinstance(c, int) else pl.multiple_of(c * ROWS, ROWS), ROWS)
-        return pltpu.make_async_copy(
-            stage.at[j, t, rows, :], (out_hbm, next_hbm)[t].at[rows, pl.ds(j * dh, dh)], out_sem.at[j, t, c]
-        )
-
     def outputs(u, t):
         j, half = divmod(u, 2)
         down = jnp.concatenate([n_d[u, s] for s in range(SUBS)], axis=0)
@@ -252,8 +246,7 @@
             if half == 0:
                 y_acc[t, rows, :] = y
             else:
-                stage[j, t, rows, :] = (y_acc[t, rows, :] + y).astype(BF16)
-                out_copy(j, t, c).start()
+                (out_ref, next_ref)[t][rows, pl.ds(j * dh, dh)] = (y_acc[t, rows, :] + y).astype(BF16)
 
     def forward_step(u, t):
         j, half = divmod(u, 2)
@@ -269,7 +262,7 @@
     for u in range(1, units):
         for c in range(chunks):
             steps[at] = functools.partial(grads_step, u, c)
-            at += 1
+            at += 2 if c == 1 else 1
     per_unit = 3 * SUBS
     for u in range(units - 1):
         at = max(at, per_unit * (u + 1) + 1)
@@ -312,9 +305,6 @@
     for j in range(hpc):
         for c in exchange[j]:
             c.wait_send()
-        for t in range(2):
-            for c in range(chunks):
-                out_copy(j, t, c).wait()
 
 
 def on_device(n, reps, keys, values, queries, next_queries, rates, tile_counts, w_gate, w_up, w_down):
@@ -328,7 +318,7 @@
     down = (units, fh, dh)
     gu_cut = (units, 2, SUBS, dh, fh // SUBS)
     down_cut = (units, SUBS, fh // SUBS, dh)
-    out = jax.ShapeDtypeStruct((tok_rows, hpc * dh), BF16)
+    out = pltpu.VMEM((tok_rows, hpc * dh), BF16)
     hbm = pl.BlockSpec(memory_space=pl.ANY)
     dma = pltpu.SemaphoreType.DMA
     pair = lambda dtype: [pltpu.VMEM(gu, dtype), pltpu.VMEM(down, dtype)]
@@ -340,20 +330,18 @@
             pl.BlockSpec(memory_space=pltpu.SMEM),
             pl.BlockSpec(memory_space=pltpu.VMEM),
         ] + [hbm] * 7,
-        out_specs=(hbm, hbm),
+        out_specs=(pl.BlockSpec(memory_space=pltpu.VMEM),) * 2,
         scratch_shapes=[
             pltpu.VMEM((hpc, 2, tok_rows, dh), BF16),
             pltpu.VMEM((hpc, 2, tok_rows, dh), BF16),
             *pair(BF16), *pair(F32), *cut(), *cut(), *cut(), *cut(),
             pltpu.VMEM((2, tok_rows, dh), F32),
             pltpu.VMEM((2, tok_rows, fh), BF16),
-            pltpu.VMEM((hpc, 2, tok_rows, dh), BF16),
             dma((hpc, 2)), dma((hpc, 2)), dma((hpc, 3)), dma((hpc, 3)), dma((hpc, 3)),
             dma((pieces,)), dma((pieces,)), dma((pieces,)), dma((pieces,)), dma((pieces,)),
-            dma((hpc, 2, tok_rows // ROWS)),
         ],
         compiler_params=pltpu.CompilerParams(
-            collective_id=0, has_side_effects=True, vmem_limit_bytes=60 * 2**20
+            collective_id=0, has_side_effects=True, vmem_limit_bytes=50 * 2**20
         ),
     )(tile_counts, rates.T, keys, values, queries, next_queries, w_gate, w_up, w_down)
 

time: 105 us -> 102 us (0.971)
  local copies, waits for them, and re-layouts: 5.69 us -> 3.33 us
  Pallas kernels: 97.9 us -> 96.7 us
    unnamed x4 -> x2, local copies, waits for them, and re-layouts: 5.69 us -> 3.33 us
    pallas_call x1, Pallas kernels: 97.9 us -> 96.7 us  [on_device(): pl.pallas_call(functools.partial(kernel, n, hpc, scale), out_shape=(out,...]
where the time goes in v3:
time: 102 us; the launch traced here: 101 us
  Pallas kernels  96.7 us (95%)
  local copies, waits for them, and re-layouts  3.33 us (3%)
  between operations  1.29 us (1%)
    pallas_call x1, Pallas kernels, on_device(): pl.pallas_call(functools.partial(kernel, n, hpc, scale), out_shape=(out,...  96.7 us
    unnamed x2, local copies, waits for them, and re-layouts  3.33 us

profile of v3, /device:TPU:0, one launch (start us, length us, event | category | flops | bytes accessed | tf_op | source)
XLA Modules:
  0.0 101.3 jit_solution(10785641600493077062)
XLA Ops:
  1.3 96.7 %shard_map.104 = (bf16[1536,1024]{1,0:T(8,128)(2,1)S(1)}, bf16[1536,1024]{1,0:T(8,128)(2,1)S(1)}) custom-call(s32[1]{0:T(128)S(6)} %copy.15.count_ref, bf16[4,1536]{1,0:T(4,128)(2,1)} %bitcast.1, bf16[1536,2048]{1,0:T(8,128)(2,1)} %k_hbm.1, bf16[1536,2048]{1,0:T(8,128)(2,1)} %v_hbm.1, bf16[1536,2048]{1,0:T(8,128)(2,1)} %q_hbm.1, bf16[1536,2048]{1,0:T(8,128)(2,1)} %qn_hbm.1, ...), custom_call_target="tpu_custom_call" | custom-call | tf_op jit(solution)/shard_map/pallas_call | solution.py:326
  98.0 1.7 %copy.13 = bf16[1536,1024]{1,0:T(8,128)(2,1)} copy(bf16[1536,1024]{1,0:T(8,128)(2,1)S(1)} %get-tuple-element.2) | data formatting | bytes 6291456
  99.7 1.7 %copy.14 = bf16[1536,1024]{1,0:T(8,128)(2,1)} copy(bf16[1536,1024]{1,0:T(8,128)(2,1)S(1)} %get-tuple-element.3) | data formatting | bytes 6291456
